TPU v7x, 32 devices: a whole 2x2x4 slice. The times are simulated.
32 devices in a mesh: samp: 16 (over z, y, x), tm: 2 (over core).
Axes of the slice: x: 2, y: 2, z: 4, core: 2. Of those that a mesh axis runs over, the one named last changes fastest.
Arguments:
- sources: bfloat16 [256, 128, 1024], P('samp', 'tm'), may hold values from -6 to 6
- operator: bfloat16 [16, 1024, 128], P(None, 'samp'), may hold values from -0.046875 to 0.046875
- lag_order: int32 [16], replicated, may hold values from 0 to 15, each once
Outputs:
- records: bfloat16 [256, 128, 128], P('samp', 'tm')
Inputs may be any that keep to these rules, and one draw needn't show every extreme that they name: `lag_order`: each lag 0 to 15 stands in exactly one slot.
All inputs are finite; a program needn't handle non-finite values.
Results may differ from a plain program's by a relative error of at most 0.001.
Values may be sent and summed in bfloat16 or wider, within the bound.
A program may use at most 64 MiB of HBM per device.

v0:
```python
import jax
import jax.numpy as jnp
from jax import lax
from jax.sharding import PartitionSpec as P


def shifted_2(block, axis, distance):
    devices = range(lax.axis_size(axis))
    route = [(i - distance, i) for i in devices if i - distance in devices]
    return lax.ppermute(block, axis, route)


def accumulate(total, piece, extended, lag_order):
    border = piece.shape[0] - 1
    window = extended.shape[1] - border
    batch = extended.shape[0]
    width = piece.shape[1]

    def step(slot, state):
        lag = lag_order[slot]
        block = lax.dynamic_index_in_dim(piece, slot, 0, keepdims=False)
        shifted = lax.dynamic_slice(extended, (0, border - lag, 0), (batch, window, width))
        return state + jnp.einsum("btj,js->bts", shifted, block, preferred_element_type=jnp.float32)

    return lax.fori_loop(0, piece.shape[0], step, total)


def per_device(sources, operator, lag_order):
    batch, window, width = sources.shape
    border = operator.shape[0] - 1
    sensors = operator.shape[2]
    tail = sources[:, window - border :, :]
    before = shifted_2(tail, "tm", 1)
    extended = jnp.concatenate([before, sources], axis=1)
    init = jnp.zeros((batch, window, sensors), jnp.float32)
    gathered = lax.all_gather(operator, "samp", axis=1, tiled=True)
    total = accumulate(init, gathered, extended, lag_order)
    return total.astype(jnp.bfloat16)


def solution(mesh):
    placed = (P("samp", "tm", None), P(None, "samp", None), P())
    return jax.shard_map(
        per_device, mesh=mesh, in_specs=placed, out_specs=P("samp", "tm", None), check_vma=False
    )
```

profile of v0, /device:TPU:0, one launch (start us, length us, event | category | flops | bytes accessed | tf_op | source)
XLA Modules:
  0.0 154.3 jit_solution(4135805747650893638)
XLA Ops:
  6.5 0.0 all-gather.2.cloned.1.call-start
  6.5 0.7 all-gather.2.cloned.1.call-update
  7.3 1.2 slice.3
  8.5 3.2 %collective-permute-start = (bf16[16,15,1024]{2,1,0:T(8,128)(2,1)S(1)}, bf16[16,15,1024]{2,1,0:T(8,128)(2,1)}, u32[]{:S(2)}, u32[]{:S(2)}) collective-permute-start(bf16[16,15,1024]{2,1,0:T(8,128)(2,1)S(1)} %slice.3), channel_id=1, source_target_pairs={{0,1},{2,3},{4,5},{6,7},{8,9},{10,11},{12,13},{14,15},{16,17},{18,... | collective-permute-start | bytes 1474568 | tf_op jit(solution)/shard_map/ppermute | solution.py:10
  11.6 0.0 copy-start
  11.6 0.8 collective-permute-done
  12.5 2.6 %pad_maximum_fusion = bf16[16,79,1024]{2,1,0:T(8,128)(2,1)S(1)} fusion(bf16[16,64,1024]{2,1,0:T(8,128)(2,1)} %param.5, bf16[16,15,1024]{2,1,0:T(8,128)(2,1)} %collective-permute-done), kind=kLoop, calls=%fused_computation.6 | loop fusion | flops 5177344 | bytes 5177344 | tf_op jit(solution)/shard_map/concatenate | solution.py:34
  15.1 74.2 %all-gather.2.cloned.1.call-done = bf16[16,1024,128]{2,1,0:T(8,128)(2,1)} async-done(((bf16[16,64,128]{2,1,0:T(8,128)(2,1)}), bf16[16,1024,128]{2,1,0:T(8,128)(2,1)}) %all-gather.2.cloned.1.call-update) | async-done | bytes 4194320 | tf_op jit(solution)/shard_map/all_gather | solution.py:36
  89.2 0.0 copy-done
  89.2 57.5 %while.16 = (s32[]{:T(128)}, f32[16,64,128]{2,1,0:T(8,128)S(1)}, s32[16]{0:T(128)S(1)}, bf16[16,79,1024]{2,1,0:T(8,128)(2,1)S(1)}, bf16[16,1024,128]{2,1,0:T(8,1...) while((s32[]{:T(128)}, f32[16,64,128]{2,1,0:T(8,128)S(1)}, s32[16]{0:T(128)S(1)}, ...), condition=%wide.region_1.2_spmd.clone, body=%wide.region_0.1_spmd.clone.sunk | while | flops 268697600 | bytes 3408549 | solution.py:25
  89.2 0.6 dynamic_slice.47
  91.1 1.7 %fusion.13 = f32[16,64,128]{2,1,0:T(8,128)S(1)} fusion(bf16[16,79,1024]{2,1,0:T(8,128)(2,1)S(1)} %get-tuple-element.218, s32[]{:T(128)S(6)} %select_n.22, f32[16,64,128]{2,1,0:T(8,128)S(1)} %get-tuple-element.207, bf16[16,1024,128]{2,1,0:T(8,128)(2,1)} %get-tuple-element.219, s32[]{:T(128)} %get-tuple-element.206, pred[]{:T(512)S(6)} %compare.3), kind=kOutput, calls=%fused_computation.2.clone.1 | convolution fusion | flops 268697600 | bytes 3408389 | tf_op jit(solution)/shard_map/while/body/eval_jaxpr/btj,js->bts/dot_general | solution.py:23
  92.8 0.6 dynamic_slice.47
  94.7 1.7 %fusion.13 = f32[16,64,128]{2,1,0:T(8,128)S(1)} fusion(bf16[16,79,1024]{2,1,0:T(8,128)(2,1)S(1)} %get-tuple-element.218, s32[]{:T(128)S(6)} %select_n.22, f32[16,64,128]{2,1,0:T(8,128)S(1)} %get-tuple-element.207, bf16[16,1024,128]{2,1,0:T(8,128)(2,1)} %get-tuple-element.219, s32[]{:T(128)} %get-tuple-element.206, pred[]{:T(512)S(6)} %compare.3), kind=kOutput, calls=%fused_computation.2.clone.1 | convolution fusion | flops 268697600 | bytes 3408389 | tf_op jit(solution)/shard_map/while/body/eval_jaxpr/btj,js->bts/dot_general | solution.py:23
  96.4 0.6 dynamic_slice.47
  98.3 1.7 %fusion.13 = f32[16,64,128]{2,1,0:T(8,128)S(1)} fusion(bf16[16,79,1024]{2,1,0:T(8,128)(2,1)S(1)} %get-tuple-element.218, s32[]{:T(128)S(6)} %select_n.22, f32[16,64,128]{2,1,0:T(8,128)S(1)} %get-tuple-element.207, bf16[16,1024,128]{2,1,0:T(8,128)(2,1)} %get-tuple-element.219, s32[]{:T(128)} %get-tuple-element.206, pred[]{:T(512)S(6)} %compare.3), kind=kOutput, calls=%fused_computation.2.clone.1 | convolution fusion | flops 268697600 | bytes 3408389 | tf_op jit(solution)/shard_map/while/body/eval_jaxpr/btj,js->bts/dot_general | solution.py:23
  100.0 0.6 dynamic_slice.47
  101.8 1.7 %fusion.13 = f32[16,64,128]{2,1,0:T(8,128)S(1)} fusion(bf16[16,79,1024]{2,1,0:T(8,128)(2,1)S(1)} %get-tuple-element.218, s32[]{:T(128)S(6)} %select_n.22, f32[16,64,128]{2,1,0:T(8,128)S(1)} %get-tuple-element.207, bf16[16,1024,128]{2,1,0:T(8,128)(2,1)} %get-tuple-element.219, s32[]{:T(128)} %get-tuple-element.206, pred[]{:T(512)S(6)} %compare.3), kind=kOutput, calls=%fused_computation.2.clone.1 | convolution fusion | flops 268697600 | bytes 3408389 | tf_op jit(solution)/shard_map/while/body/eval_jaxpr/btj,js->bts/dot_general | solution.py:23
  103.6 0.6 dynamic_slice.47
  105.4 1.7 %fusion.13 = f32[16,64,128]{2,1,0:T(8,128)S(1)} fusion(bf16[16,79,1024]{2,1,0:T(8,128)(2,1)S(1)} %get-tuple-element.218, s32[]{:T(128)S(6)} %select_n.22, f32[16,64,128]{2,1,0:T(8,128)S(1)} %get-tuple-element.207, bf16[16,1024,128]{2,1,0:T(8,128)(2,1)} %get-tuple-element.219, s32[]{:T(128)} %get-tuple-element.206, pred[]{:T(512)S(6)} %compare.3), kind=kOutput, calls=%fused_computation.2.clone.1 | convolution fusion | flops 268697600 | bytes 3408389 | tf_op jit(solution)/shard_map/while/body/eval_jaxpr/btj,js->bts/dot_general | solution.py:23
  107.2 0.6 dynamic_slice.47
  109.0 1.7 %fusion.13 = f32[16,64,128]{2,1,0:T(8,128)S(1)} fusion(bf16[16,79,1024]{2,1,0:T(8,128)(2,1)S(1)} %get-tuple-element.218, s32[]{:T(128)S(6)} %select_n.22, f32[16,64,128]{2,1,0:T(8,128)S(1)} %get-tuple-element.207, bf16[16,1024,128]{2,1,0:T(8,128)(2,1)} %get-tuple-element.219, s32[]{:T(128)} %get-tuple-element.206, pred[]{:T(512)S(6)} %compare.3), kind=kOutput, calls=%fused_computation.2.clone.1 | convolution fusion | flops 268697600 | bytes 3408389 | tf_op jit(solution)/shard_map/while/body/eval_jaxpr/btj,js->bts/dot_general | solution.py:23
  110.8 0.6 dynamic_slice.47
  112.6 1.7 %fusion.13 = f32[16,64,128]{2,1,0:T(8,128)S(1)} fusion(bf16[16,79,1024]{2,1,0:T(8,128)(2,1)S(1)} %get-tuple-element.218, s32[]{:T(128)S(6)} %select_n.22, f32[16,64,128]{2,1,0:T(8,128)S(1)} %get-tuple-element.207, bf16[16,1024,128]{2,1,0:T(8,128)(2,1)} %get-tuple-element.219, s32[]{:T(128)} %get-tuple-element.206, pred[]{:T(512)S(6)} %compare.3), kind=kOutput, calls=%fused_computation.2.clone.1 | convolution fusion | flops 268697600 | bytes 3408389 | tf_op jit(solution)/shard_map/while/body/eval_jaxpr/btj,js->bts/dot_general | solution.py:23
  114.4 0.6 dynamic_slice.47
  116.2 1.7 %fusion.13 = f32[16,64,128]{2,1,0:T(8,128)S(1)} fusion(bf16[16,79,1024]{2,1,0:T(8,128)(2,1)S(1)} %get-tuple-element.218, s32[]{:T(128)S(6)} %select_n.22, f32[16,64,128]{2,1,0:T(8,128)S(1)} %get-tuple-element.207, bf16[16,1024,128]{2,1,0:T(8,128)(2,1)} %get-tuple-element.219, s32[]{:T(128)} %get-tuple-element.206, pred[]{:T(512)S(6)} %compare.3), kind=kOutput, calls=%fused_computation.2.clone.1 | convolution fusion | flops 268697600 | bytes 3408389 | tf_op jit(solution)/shard_map/while/body/eval_jaxpr/btj,js->bts/dot_general | solution.py:23
  118.0 0.6 dynamic_slice.47
  119.8 1.7 %fusion.13 = f32[16,64,128]{2,1,0:T(8,128)S(1)} fusion(bf16[16,79,1024]{2,1,0:T(8,128)(2,1)S(1)} %get-tuple-element.218, s32[]{:T(128)S(6)} %select_n.22, f32[16,64,128]{2,1,0:T(8,128)S(1)} %get-tuple-element.207, bf16[16,1024,128]{2,1,0:T(8,128)(2,1)} %get-tuple-element.219, s32[]{:T(128)} %get-tuple-element.206, pred[]{:T(512)S(6)} %compare.3), kind=kOutput, calls=%fused_computation.2.clone.1 | convolution fusion | flops 268697600 | bytes 3408389 | tf_op jit(solution)/shard_map/while/body/eval_jaxpr/btj,js->bts/dot_general | solution.py:23
  121.6 0.6 dynamic_slice.47
  123.4 1.7 %fusion.13 = f32[16,64,128]{2,1,0:T(8,128)S(1)} fusion(bf16[16,79,1024]{2,1,0:T(8,128)(2,1)S(1)} %get-tuple-element.218, s32[]{:T(128)S(6)} %select_n.22, f32[16,64,128]{2,1,0:T(8,128)S(1)} %get-tuple-element.207, bf16[16,1024,128]{2,1,0:T(8,128)(2,1)} %get-tuple-element.219, s32[]{:T(128)} %get-tuple-element.206, pred[]{:T(512)S(6)} %compare.3), kind=kOutput, calls=%fused_computation.2.clone.1 | convolution fusion | flops 268697600 | bytes 3408389 | tf_op jit(solution)/shard_map/while/body/eval_jaxpr/btj,js->bts/dot_general | solution.py:23
  125.2 0.6 dynamic_slice.47
  127.0 1.7 %fusion.13 = f32[16,64,128]{2,1,0:T(8,128)S(1)} fusion(bf16[16,79,1024]{2,1,0:T(8,128)(2,1)S(1)} %get-tuple-element.218, s32[]{:T(128)S(6)} %select_n.22, f32[16,64,128]{2,1,0:T(8,128)S(1)} %get-tuple-element.207, bf16[16,1024,128]{2,1,0:T(8,128)(2,1)} %get-tuple-element.219, s32[]{:T(128)} %get-tuple-element.206, pred[]{:T(512)S(6)} %compare.3), kind=kOutput, calls=%fused_computation.2.clone.1 | convolution fusion | flops 268697600 | bytes 3408389 | tf_op jit(solution)/shard_map/while/body/eval_jaxpr/btj,js->bts/dot_general | solution.py:23
  128.8 0.6 dynamic_slice.47
  130.6 1.7 %fusion.13 = f32[16,64,128]{2,1,0:T(8,128)S(1)} fusion(bf16[16,79,1024]{2,1,0:T(8,128)(2,1)S(1)} %get-tuple-element.218, s32[]{:T(128)S(6)} %select_n.22, f32[16,64,128]{2,1,0:T(8,128)S(1)} %get-tuple-element.207, bf16[16,1024,128]{2,1,0:T(8,128)(2,1)} %get-tuple-element.219, s32[]{:T(128)} %get-tuple-element.206, pred[]{:T(512)S(6)} %compare.3), kind=kOutput, calls=%fused_computation.2.clone.1 | convolution fusion | flops 268697600 | bytes 3408389 | tf_op jit(solution)/shard_map/while/body/eval_jaxpr/btj,js->bts/dot_general | solution.py:23
  132.4 0.6 dynamic_slice.47
  134.2 1.7 %fusion.13 = f32[16,64,128]{2,1,0:T(8,128)S(1)} fusion(bf16[16,79,1024]{2,1,0:T(8,128)(2,1)S(1)} %get-tuple-element.218, s32[]{:T(128)S(6)} %select_n.22, f32[16,64,128]{2,1,0:T(8,128)S(1)} %get-tuple-element.207, bf16[16,1024,128]{2,1,0:T(8,128)(2,1)} %get-tuple-element.219, s32[]{:T(128)} %get-tuple-element.206, pred[]{:T(512)S(6)} %compare.3), kind=kOutput, calls=%fused_computation.2.clone.1 | convolution fusion | flops 268697600 | bytes 3408389 | tf_op jit(solution)/shard_map/while/body/eval_jaxpr/btj,js->bts/dot_general | solution.py:23
  136.0 0.6 dynamic_slice.47
  137.8 1.7 %fusion.13 = f32[16,64,128]{2,1,0:T(8,128)S(1)} fusion(bf16[16,79,1024]{2,1,0:T(8,128)(2,1)S(1)} %get-tuple-element.218, s32[]{:T(128)S(6)} %select_n.22, f32[16,64,128]{2,1,0:T(8,128)S(1)} %get-tuple-element.207, bf16[16,1024,128]{2,1,0:T(8,128)(2,1)} %get-tuple-element.219, s32[]{:T(128)} %get-tuple-element.206, pred[]{:T(512)S(6)} %compare.3), kind=kOutput, calls=%fused_computation.2.clone.1 | convolution fusion | flops 268697600 | bytes 3408389 | tf_op jit(solution)/shard_map/while/body/eval_jaxpr/btj,js->bts/dot_general | solution.py:23
  139.6 0.6 dynamic_slice.47
  141.4 1.7 %fusion.13 = f32[16,64,128]{2,1,0:T(8,128)S(1)} fusion(bf16[16,79,1024]{2,1,0:T(8,128)(2,1)S(1)} %get-tuple-element.218, s32[]{:T(128)S(6)} %select_n.22, f32[16,64,128]{2,1,0:T(8,128)S(1)} %get-tuple-element.207, bf16[16,1024,128]{2,1,0:T(8,128)(2,1)} %get-tuple-element.219, s32[]{:T(128)} %get-tuple-element.206, pred[]{:T(512)S(6)} %compare.3), kind=kOutput, calls=%fused_computation.2.clone.1 | convolution fusion | flops 268697600 | bytes 3408389 | tf_op jit(solution)/shard_map/while/body/eval_jaxpr/btj,js->bts/dot_general | solution.py:23
  143.2 0.6 dynamic_slice.47
  145.0 1.7 %fusion.13 = f32[16,64,128]{2,1,0:T(8,128)S(1)} fusion(bf16[16,79,1024]{2,1,0:T(8,128)(2,1)S(1)} %get-tuple-element.218, s32[]{:T(128)S(6)} %select_n.22, f32[16,64,128]{2,1,0:T(8,128)S(1)} %get-tuple-element.207, bf16[16,1024,128]{2,1,0:T(8,128)(2,1)} %get-tuple-element.219, s32[]{:T(128)} %get-tuple-element.206, pred[]{:T(512)S(6)} %compare.3), kind=kOutput, calls=%fused_computation.2.clone.1 | convolution fusion | flops 268697600 | bytes 3408389 | tf_op jit(solution)/shard_map/while/body/eval_jaxpr/btj,js->bts/dot_general | solution.py:23
  146.8 0.7 convert_element_type.3
  (1 shorter events, 0.0 us)
Async XLA Ops:
  6.5 82.7 %all-gather.2.cloned.1.call-start = ((), (), s32[]{:S(2)}) async-start(), calls=%async_computation | async-start | bytes 4456448 | tf_op jit(solution)/shard_map/all_gather | solution.py:36
  8.5 4.0 %collective-permute-start = (bf16[16,15,1024]{2,1,0:T(8,128)(2,1)S(1)}, bf16[16,15,1024]{2,1,0:T(8,128)(2,1)}, u32[]{:S(2)}, u32[]{:S(2)}) collective-permute-start(bf16[16,15,1024]{2,1,0:T(8,128)(2,1)S(1)} %slice.3), channel_id=1, source_target_pairs={{0,1},{2,3},{4,5},{6,7},{8,9},{10,11},{12,13},{14,15},{16,17},{18,... | collective-permute-start | bytes 1474568 | tf_op jit(solution)/shard_map/ppermute | solution.py:10
  11.6 77.6 %copy-start = (s32[16]{0:T(128)S(1)}, s32[16]{0:T(128)}, u32[]{:S(2)}) copy-start(s32[16]{0:T(128)} %param.7) | copy-start | bytes 196
Sparse Core Ops, SparseCore 0:
  10.1 79.0 all-gather.1
where the time goes:
time: 155 us; the launch traced here: 154 us
  waiting for transfers between devices  75.7 us (49%)
  matrix products  27.8 us (18%)
  loops' own time  20.2 us (13%)
  between operations  13.4 us (9%)
  local copies, waits for them, and re-layouts  10.7 us (7%)
  other arithmetic  3.33 us (2%)
  starting transfers between devices  3.18 us (2%)
    all_gather x1, waiting for transfers between devices, per_device(): gathered = lax.all_gather(operator, 'samp', axis=1, tiled=True)  74.2 us
    dot_general x16, matrix products, step(): jnp.einsum('btj,js->bts', shifted, block, preferred_element_type=jnp.floa...  27.8 us
    another operation x1, loops' own time, accumulate(): return lax.fori_loop(0, piece.shape[0], step, total)  20.2 us
    dynamic_slice x16, local copies, waits for them, and re-layouts, step(): lag = lag_order[slot]  9.47 us
    ppermute x1, starting transfers between devices, shifted_2(): return lax.ppermute(block, axis, route)  3.17 us
  transfers between devices with their start and end apart: 2, of which 2 were waited for; matrix products, arithmetic and copies ran while one was open for 2% of the time, Pallas kernels for 0%

commit v1 on v0

--- a/solution.py
+++ b/solution.py
@@ -33,7 +33,23 @@
     before = shifted_2(tail, "tm", 1)
     extended = jnp.concatenate([before, sources], axis=1)
     init = jnp.zeros((batch, window, sensors), jnp.float32)
-    gathered = lax.all_gather(operator, "samp", axis=1, tiled=True)
+    ways, here, lap = (lax.axis_size("samp"), lax.axis_index("samp"), operator.shape[1])
+    lengths = [n * ways if d == 1 else n for d, n in enumerate(operator.shape)]
+    full = lax.dynamic_update_slice_in_dim(
+        jnp.zeros(lengths, operator.dtype), operator, here * lap, axis=1
+    )
+    going_up = going_down = operator
+    for far in range(1, ways // 2 + 1):
+        going_up = lax.ppermute(going_up, "samp", [(d, (d + 1) % ways) for d in range(ways)])
+        full = lax.dynamic_update_slice_in_dim(full, going_up, (here - far) % ways * lap, axis=1)
+        if 2 * far < ways:
+            going_down = lax.ppermute(
+                going_down, "samp", [(d, (d - 1) % ways) for d in range(ways)]
+            )
+            full = lax.dynamic_update_slice_in_dim(
+                full, going_down, (here + far) % ways * lap, axis=1
+            )
+    gathered = full
     total = accumulate(init, gathered, extended, lag_order)
     return total.astype(jnp.bfloat16)
 

time: 155 us -> 162 us (1.045)
  starting transfers between devices: 3.18 us -> 57.6 us
  waiting for transfers between devices: 75.7 us -> 22.6 us
  local copies, waits for them, and re-layouts: 10.7 us -> 27.5 us
  between operations: 13.4 us -> 0.06 us
    all_gather x1 -> x0, waiting for transfers between devices: 74.2 us -> none  [per_device(): gathered = lax.all_gather(operator, 'samp', axis=1, tiled=True)]
    ppermute x0 -> x15, starting transfers between devices: none -> 55.4 us  [the longest x7 38.4 us: per_device(): lax.ppermute(going_down, 'samp', [(d, (d - 1) % ways) for d in range(ways)])]
    ppermute x0 -> x15, waiting for transfers between devices: none -> 22.6 us  [the longest x8 18.4 us: per_device(): lax.ppermute(going_up, 'samp', [(d, (d + 1) % ways) for d in range(ways)])]
    dynamic_update_slice x0 -> x16, local copies, waits for them, and re-layouts: none -> 14.2 us  [the longest x8 7.12 us: per_device(): lax.dynamic_update_slice_in_dim(full, going_up, (here - far) % ways * lap...]
    broadcast_in_dim x0 -> x1, local copies, waits for them, and re-layouts: none -> 2.76 us  [per_device(): jnp.zeros(lengths, operator.dtype)]
  transfers between devices with their start and end apart: 2 -> 16, of which waited for: 2 -> 7; matrix products, arithmetic and copies ran while one was open for 2% -> 12% of each run, Pallas kernels for 0% -> 0%
where the time goes in v1:
time: 162 us; the launch traced here: 160 us
  starting transfers between devices  57.6 us (36%)
  matrix products  27.8 us (17%)
  local copies, waits for them, and re-layouts  27.5 us (17%)
  waiting for transfers between devices  22.6 us (14%)
  loops' own time  21.2 us (13%)
  other arithmetic  3.38 us (2%)
    ppermute x7, starting transfers between devices, per_device(): lax.ppermute(going_down, 'samp', [(d, (d - 1) % ways) for d in range(ways)])  38.4 us
    dot_general x16, matrix products, step(): jnp.einsum('btj,js->bts', shifted, block, preferred_element_type=jnp.floa...  27.8 us
    another operation x1, loops' own time, accumulate(): return lax.fori_loop(0, piece.shape[0], step, total)  21.2 us
    ppermute x8, waiting for transfers between devices, per_device(): lax.ppermute(going_up, 'samp', [(d, (d + 1) % ways) for d in range(ways)])  18.4 us
    ppermute x8, starting transfers between devices, per_device(): lax.ppermute(going_up, 'samp', [(d, (d + 1) % ways) for d in range(ways)])  17 us
    dynamic_slice x16, local copies, waits for them, and re-layouts, step(): lag = lag_order[slot]  9.38 us
    dynamic_update_slice x8, local copies, waits for them, and re-layouts, per_device(): lax.dynamic_update_slice_in_dim(full, going_up, (here - far) % ways * lap...  7.12 us
    dynamic_update_slice x7, local copies, waits for them, and re-layouts, per_device(): lax.dynamic_update_slice_in_dim(full, going_down, (here + far) % ways * l...  6.32 us
  transfers between devices with their start and end apart: 16, of which 7 were waited for; matrix products, arithmetic and copies ran while one was open for 12% of the time, Pallas kernels for 0%

profile of v1, /device:TPU:0, one launch (start us, length us, event | category | flops | bytes accessed | tf_op | source)
XLA Modules:
  0.0 160.2 jit_solution(10624334689797624918)
XLA Ops:
  0.0 2.9 %collective-permute-start.1 = (bf16[16,64,128]{2,1,0:T(8,128)(2,1)}, bf16[16,64,128]{2,1,0:T(8,128)(2,1)S(1)}, u32[]{:S(2)}, u32[]{:S(2)}) collective-permute-start(bf16[16,64,128]{2,1,0:T(8,128)(2,1)} %param.6), channel_id=1, source_target_pairs={{0,2},{2,4},{4,6},{6,8},{8,10},{10,12},{12,14},{14,16},{16,18},{18... | collective-permute-start | bytes 786440 | tf_op jit(solution)/shard_map/ppermute | solution.py:43
  2.9 4.0 %collective-permute-start.2 = (bf16[16,64,128]{2,1,0:T(8,128)(2,1)}, bf16[16,64,128]{2,1,0:T(8,128)(2,1)S(1)}, u32[]{:S(2)}, u32[]{:S(2)}) collective-permute-start(bf16[16,64,128]{2,1,0:T(8,128)(2,1)} %param.6), channel_id=1, source_target_pairs={{0,30},{2,0},{4,2},{6,4},{8,6},{10,8},{12,10},{14,12},{16,14},{18,... | collective-permute-start | bytes 786440 | tf_op jit(solution)/shard_map/ppermute | solution.py:46
  7.0 7.5 %collective-permute-done.1 = bf16[16,64,128]{2,1,0:T(8,128)(2,1)S(1)} collective-permute-done((bf16[16,64,128]{2,1,0:T(8,128)(2,1)}, bf16[16,64,128]{2,1,0:T(8,128)(2,1)S(1)}, u32[]{:S(2)}, u32[]{:S(2)}) %collective-permute-start.1) | collective-permute-done | bytes 262176 | tf_op jit(solution)/shard_map/ppermute | solution.py:43
  14.4 2.4 %collective-permute-start.3 = (bf16[16,64,128]{2,1,0:T(8,128)(2,1)S(1)}, bf16[16,64,128]{2,1,0:T(8,128)(2,1)S(1)}, u32[]{:S(2)}, u32[]{:S(2)}) collective-permute-start(bf16[16,64,128]{2,1,0:T(8,128)(2,1)S(1)} %collective-permute-done.1), channel_id=1, source_target_pairs={{0,2},{2,4},{4,6},{6,8},{8,10},{10,12},{12,14},{14,16},{16,18},{18... | collective-permute-start | bytes 786440 | tf_op jit(solution)/shard_map/ppermute | solution.py:43
  16.8 3.2 %collective-permute-start.4 = (bf16[16,64,128]{2,1,0:T(8,128)(2,1)S(1)}, bf16[16,64,128]{2,1,0:T(8,128)(2,1)S(1)}, u32[]{:S(2)}, u32[]{:S(2)}) collective-permute-start(bf16[16,64,128]{2,1,0:T(8,128)(2,1)S(1)} %collective-permute-done.2), channel_id=1, source_target_pairs={{0,30},{2,0},{4,2},{6,4},{8,6},{10,8},{12,10},{14,12},{16,14},{18,... | collective-permute-start | bytes 786440 | tf_op jit(solution)/shard_map/ppermute | solution.py:46
  20.1 1.2 slice.3
  21.3 2.2 %collective-permute-start = (bf16[16,15,1024]{2,1,0:T(8,128)(2,1)S(1)}, bf16[16,15,1024]{2,1,0:T(8,128)(2,1)}, u32[]{:S(2)}, u32[]{:S(2)}) collective-permute-start(bf16[16,15,1024]{2,1,0:T(8,128)(2,1)S(1)} %slice.3), channel_id=1, source_target_pairs={{0,1},{2,3},{4,5},{6,7},{8,9},{10,11},{12,13},{14,15},{16,17},{18,... | collective-permute-start | bytes 1474568 | tf_op jit(solution)/shard_map/ppermute | solution.py:10
  23.5 3.7 %collective-permute-done.3 = bf16[16,64,128]{2,1,0:T(8,128)(2,1)S(1)} collective-permute-done((bf16[16,64,128]{2,1,0:T(8,128)(2,1)S(1)}, bf16[16,64,128]{2,1,0:T(8,128)(2,1)S(1)}, u32[]{:S(2)}, u32[]{:S(2)}) %collective-permute-start.3) | collective-permute-done | bytes 262176 | tf_op jit(solution)/shard_map/ppermute | solution.py:43
  27.1 2.5 %collective-permute-start.5 = (bf16[16,64,128]{2,1,0:T(8,128)(2,1)S(1)}, bf16[16,64,128]{2,1,0:T(8,128)(2,1)}, u32[]{:S(2)}, u32[]{:S(2)}) collective-permute-start(bf16[16,64,128]{2,1,0:T(8,128)(2,1)S(1)} %collective-permute-done.3), channel_id=1, source_target_pairs={{0,2},{2,4},{4,6},{6,8},{8,10},{10,12},{12,14},{14,16},{16,18},{18... | collective-permute-start | bytes 786440 | tf_op jit(solution)/shard_map/ppermute | solution.py:43
  29.6 4.7 %collective-permute-start.6 = (bf16[16,64,128]{2,1,0:T(8,128)(2,1)S(1)}, bf16[16,64,128]{2,1,0:T(8,128)(2,1)}, u32[]{:S(2)}, u32[]{:S(2)}) collective-permute-start(bf16[16,64,128]{2,1,0:T(8,128)(2,1)S(1)} %collective-permute-done.4), channel_id=1, source_target_pairs={{0,30},{2,0},{4,2},{6,4},{8,6},{10,8},{12,10},{14,12},{16,14},{18,... | collective-permute-start | bytes 786440 | tf_op jit(solution)/shard_map/ppermute | solution.py:46
  34.3 2.8 %broadcast_in_dim.7 = bf16[16,1024,128]{2,1,0:T(8,128)(2,1)} broadcast(bf16[]{:T(256)} %constant.152.clone.1), dimensions={} | broadcast | bytes 4194306 | tf_op jit(solution)/shard_map/broadcast_in_dim | solution.py:39
  37.8 0.8 constant_dynamic-update-slice_fusion.14
  39.0 2.6 %collective-permute-start.7 = (bf16[16,64,128]{2,1,0:T(8,128)(2,1)}, bf16[16,64,128]{2,1,0:T(8,128)(2,1)S(1)}, u32[]{:S(2)}, u32[]{:S(2)}) collective-permute-start(bf16[16,64,128]{2,1,0:T(8,128)(2,1)} %collective-permute-done.5), channel_id=1, source_target_pairs={{0,2},{2,4},{4,6},{6,8},{8,10},{10,12},{12,14},{14,16},{16,18},{18... | collective-permute-start | bytes 786440 | tf_op jit(solution)/shard_map/ppermute | solution.py:43
  42.3 5.7 %collective-permute-start.8 = (bf16[16,64,128]{2,1,0:T(8,128)(2,1)}, bf16[16,64,128]{2,1,0:T(8,128)(2,1)S(1)}, u32[]{:S(2)}, u32[]{:S(2)}) collective-permute-start(bf16[16,64,128]{2,1,0:T(8,128)(2,1)} %collective-permute-done.6), channel_id=1, source_target_pairs={{0,30},{2,0},{4,2},{6,4},{8,6},{10,8},{12,10},{14,12},{16,14},{18,... | collective-permute-start | bytes 786440 | tf_op jit(solution)/shard_map/ppermute | solution.py:46
  48.1 2.6 %pad_maximum_fusion = bf16[16,79,1024]{2,1,0:T(8,128)(2,1)S(1)} fusion(bf16[16,64,1024]{2,1,0:T(8,128)(2,1)} %param.5, bf16[16,15,1024]{2,1,0:T(8,128)(2,1)} %collective-permute-done), kind=kLoop, calls=%fused_computation.6 | loop fusion | flops 5177344 | bytes 5177344 | tf_op jit(solution)/shard_map/concatenate | solution.py:34
  50.7 1.0 collective-permute-done.7
  51.7 2.4 %collective-permute-start.9 = (bf16[16,64,128]{2,1,0:T(8,128)(2,1)S(1)}, bf16[16,64,128]{2,1,0:T(8,128)(2,1)S(1)}, u32[]{:S(2)}, u32[]{:S(2)}) collective-permute-start(bf16[16,64,128]{2,1,0:T(8,128)(2,1)S(1)} %collective-permute-done.7), channel_id=1, source_target_pairs={{0,2},{2,4},{4,6},{6,8},{8,10},{10,12},{12,14},{14,16},{16,18},{18... | collective-permute-start | bytes 786440 | tf_op jit(solution)/shard_map/ppermute | solution.py:43
  54.1 0.8 constant_dynamic-update-slice_fusion.12
  54.9 0.8 constant_dynamic-update-slice_fusion.11
  55.7 6.7 %collective-permute-start.10 = (bf16[16,64,128]{2,1,0:T(8,128)(2,1)S(1)}, bf16[16,64,128]{2,1,0:T(8,128)(2,1)S(1)}, u32[]{:S(2)}, u32[]{:S(2)}) collective-permute-start(bf16[16,64,128]{2,1,0:T(8,128)(2,1)S(1)} %collective-permute-done.8), channel_id=1, source_target_pairs={{0,30},{2,0},{4,2},{6,4},{8,6},{10,8},{12,10},{14,12},{16,14},{18,... | collective-permute-start | bytes 786440 | tf_op jit(solution)/shard_map/ppermute | solution.py:46
  62.3 1.7 %constant_dynamic-update-slice_fusion.10 = bf16[16,1024,128]{2,1,0:T(8,128)(2,1)} fusion(bf16[16,1024,128]{2,1,0:T(8,128)(2,1)} %constant_dynamic-update-slice_fusion.11, bf16[16,64,128]{2,1,0:T(8,128)(2,1)} %collective-permute-done.5, s32[]{:T(128)S(6)} %select_n.141), kind=kLoop, calls=%fused_computation.17 | loop fusion | bytes 524292 | tf_op jit(solution)/shard_map/dynamic_update_slice | solution.py:44
  64.1 2.0 %collective-permute-start.11 = (bf16[16,64,128]{2,1,0:T(8,128)(2,1)S(1)}, bf16[16,64,128]{2,1,0:T(8,128)(2,1)S(1)}, u32[]{:S(2)}, u32[]{:S(2)}) collective-permute-start(bf16[16,64,128]{2,1,0:T(8,128)(2,1)S(1)} %collective-permute-done.9), channel_id=1, source_target_pairs={{0,2},{2,4},{4,6},{6,8},{8,10},{10,12},{12,14},{14,16},{16,18},{18... | collective-permute-start | bytes 786440 | tf_op jit(solution)/shard_map/ppermute | solution.py:43
  66.1 1.7 %constant_dynamic-update-slice_fusion.9 = bf16[16,1024,128]{2,1,0:T(8,128)(2,1)} fusion(bf16[16,1024,128]{2,1,0:T(8,128)(2,1)} %constant_dynamic-update-slice_fusion.10, bf16[16,64,128]{2,1,0:T(8,128)(2,1)} %collective-permute-done.6, s32[]{:T(128)S(6)} %select_n.143), kind=kLoop, calls=%fused_computation.16 | loop fusion | bytes 524292 | tf_op jit(solution)/shard_map/dynamic_update_slice | solution.py:49
  68.6 7.3 %collective-permute-start.12 = (bf16[16,64,128]{2,1,0:T(8,128)(2,1)S(1)}, bf16[16,64,128]{2,1,0:T(8,128)(2,1)S(1)}, u32[]{:S(2)}, u32[]{:S(2)}) collective-permute-start(bf16[16,64,128]{2,1,0:T(8,128)(2,1)S(1)} %collective-permute-done.10), channel_id=1, source_target_pairs={{0,30},{2,0},{4,2},{6,4},{8,6},{10,8},{12,10},{14,12},{16,14},{18,... | collective-permute-start | bytes 786440 | tf_op jit(solution)/shard_map/ppermute | solution.py:46
  77.4 0.8 constant_dynamic-update-slice_fusion.5
  78.2 3.0 %collective-permute-done.12 = bf16[16,64,128]{2,1,0:T(8,128)(2,1)S(1)} collective-permute-done((bf16[16,64,128]{2,1,0:T(8,128)(2,1)S(1)}, bf16[16,64,128]{2,1,0:T(8,128)(2,1)S(1)}, u32[]{:S(2)}, u32[]{:S(2)}) %collective-permute-start.12) | collective-permute-done | bytes 262176 | tf_op jit(solution)/shard_map/ppermute | solution.py:46
  81.2 6.8 %collective-permute-start.14 = (bf16[16,64,128]{2,1,0:T(8,128)(2,1)S(1)}, bf16[16,64,128]{2,1,0:T(8,128)(2,1)S(1)}, u32[]{:S(2)}, u32[]{:S(2)}) collective-permute-start(bf16[16,64,128]{2,1,0:T(8,128)(2,1)S(1)} %collective-permute-done.12), channel_id=1, source_target_pairs={{0,30},{2,0},{4,2},{6,4},{8,6},{10,8},{12,10},{14,12},{16,14},{18,... | collective-permute-start | bytes 786440 | tf_op jit(solution)/shard_map/ppermute | solution.py:46
  88.7 2.2 %collective-permute-start.15 = (bf16[16,64,128]{2,1,0:T(8,128)(2,1)S(1)}, bf16[16,64,128]{2,1,0:T(8,128)(2,1)S(1)}, u32[]{:S(2)}, u32[]{:S(2)}) collective-permute-start(bf16[16,64,128]{2,1,0:T(8,128)(2,1)S(1)} %collective-permute-done.13), channel_id=1, source_target_pairs={{0,2},{2,4},{4,6},{6,8},{8,10},{10,12},{12,14},{14,16},{16,18},{18... | collective-permute-start | bytes 786440 | tf_op jit(solution)/shard_map/ppermute | solution.py:43
  91.7 0.8 constant_dynamic-update-slice_fusion.2
  92.5 1.2 collective-permute-done.14
  94.4 5.8 %collective-permute-done.15 = bf16[16,64,128]{2,1,0:T(8,128)(2,1)S(1)} collective-permute-done((bf16[16,64,128]{2,1,0:T(8,128)(2,1)S(1)}, bf16[16,64,128]{2,1,0:T(8,128)(2,1)S(1)}, u32[]{:S(2)}, u32[]{:S(2)}) %collective-permute-start.15) | collective-permute-done | bytes 262176 | tf_op jit(solution)/shard_map/ppermute | solution.py:43
  101.0 58.5 %while.16 = (s32[]{:T(128)}, f32[16,64,128]{2,1,0:T(8,128)S(1)}, s32[16]{0:T(128)S(1)}, bf16[16,79,1024]{2,1,0:T(8,128)(2,1)S(1)}, bf16[16,1024,128]{2,1,0:T(8,1...) while((s32[]{:T(128)}, f32[16,64,128]{2,1,0:T(8,128)S(1)}, s32[16]{0:T(128)S(1)}, ...), condition=%wide.region_1.2_spmd.clone, body=%wide.region_0.1_spmd.clone.sunk | while | flops 268697600 | bytes 3408549 | solution.py:25
  102.9 1.7 %fusion.13 = f32[16,64,128]{2,1,0:T(8,128)S(1)} fusion(bf16[16,79,1024]{2,1,0:T(8,128)(2,1)S(1)} %get-tuple-element.218, s32[]{:T(128)S(6)} %select_n.164, f32[16,64,128]{2,1,0:T(8,128)S(1)} %get-tuple-element.207, bf16[16,1024,128]{2,1,0:T(8,128)(2,1)} %get-tuple-element.219, s32[]{:T(128)} %get-tuple-element.206, pred[]{:T(512)S(6)} %compare.18), kind=kOutput, calls=%fused_computation.2.clone.1 | convolution fusion | flops 268697600 | bytes 3408389 | tf_op jit(solution)/shard_map/while/body/eval_jaxpr/btj,js->bts/dot_general | solution.py:23
  106.6 1.7 %fusion.13 = f32[16,64,128]{2,1,0:T(8,128)S(1)} fusion(bf16[16,79,1024]{2,1,0:T(8,128)(2,1)S(1)} %get-tuple-element.218, s32[]{:T(128)S(6)} %select_n.164, f32[16,64,128]{2,1,0:T(8,128)S(1)} %get-tuple-element.207, bf16[16,1024,128]{2,1,0:T(8,128)(2,1)} %get-tuple-element.219, s32[]{:T(128)} %get-tuple-element.206, pred[]{:T(512)S(6)} %compare.18), kind=kOutput, calls=%fused_computation.2.clone.1 | convolution fusion | flops 268697600 | bytes 3408389 | tf_op jit(solution)/shard_map/while/body/eval_jaxpr/btj,js->bts/dot_general | solution.py:23
  110.2 1.7 %fusion.13 = f32[16,64,128]{2,1,0:T(8,128)S(1)} fusion(bf16[16,79,1024]{2,1,0:T(8,128)(2,1)S(1)} %get-tuple-element.218, s32[]{:T(128)S(6)} %select_n.164, f32[16,64,128]{2,1,0:T(8,128)S(1)} %get-tuple-element.207, bf16[16,1024,128]{2,1,0:T(8,128)(2,1)} %get-tuple-element.219, s32[]{:T(128)} %get-tuple-element.206, pred[]{:T(512)S(6)} %compare.18), kind=kOutput, calls=%fused_computation.2.clone.1 | convolution fusion | flops 268697600 | bytes 3408389 | tf_op jit(solution)/shard_map/while/body/eval_jaxpr/btj,js->bts/dot_general | solution.py:23
  113.9 1.7 %fusion.13 = f32[16,64,128]{2,1,0:T(8,128)S(1)} fusion(bf16[16,79,1024]{2,1,0:T(8,128)(2,1)S(1)} %get-tuple-element.218, s32[]{:T(128)S(6)} %select_n.164, f32[16,64,128]{2,1,0:T(8,128)S(1)} %get-tuple-element.207, bf16[16,1024,128]{2,1,0:T(8,128)(2,1)} %get-tuple-element.219, s32[]{:T(128)} %get-tuple-element.206, pred[]{:T(512)S(6)} %compare.18), kind=kOutput, calls=%fused_computation.2.clone.1 | convolution fusion | flops 268697600 | bytes 3408389 | tf_op jit(solution)/shard_map/while/body/eval_jaxpr/btj,js->bts/dot_general | solution.py:23
  117.5 1.7 %fusion.13 = f32[16,64,128]{2,1,0:T(8,128)S(1)} fusion(bf16[16,79,1024]{2,1,0:T(8,128)(2,1)S(1)} %get-tuple-element.218, s32[]{:T(128)S(6)} %select_n.164, f32[16,64,128]{2,1,0:T(8,128)S(1)} %get-tuple-element.207, bf16[16,1024,128]{2,1,0:T(8,128)(2,1)} %get-tuple-element.219, s32[]{:T(128)} %get-tuple-element.206, pred[]{:T(512)S(6)} %compare.18), kind=kOutput, calls=%fused_computation.2.clone.1 | convolution fusion | flops 268697600 | bytes 3408389 | tf_op jit(solution)/shard_map/while/body/eval_jaxpr/btj,js->bts/dot_general | solution.py:23
  121.2 1.7 %fusion.13 = f32[16,64,128]{2,1,0:T(8,128)S(1)} fusion(bf16[16,79,1024]{2,1,0:T(8,128)(2,1)S(1)} %get-tuple-element.218, s32[]{:T(128)S(6)} %select_n.164, f32[16,64,128]{2,1,0:T(8,128)S(1)} %get-tuple-element.207, bf16[16,1024,128]{2,1,0:T(8,128)(2,1)} %get-tuple-element.219, s32[]{:T(128)} %get-tuple-element.206, pred[]{:T(512)S(6)} %compare.18), kind=kOutput, calls=%fused_computation.2.clone.1 | convolution fusion | flops 268697600 | bytes 3408389 | tf_op jit(solution)/shard_map/while/body/eval_jaxpr/btj,js->bts/dot_general | solution.py:23
  124.8 1.7 %fusion.13 = f32[16,64,128]{2,1,0:T(8,128)S(1)} fusion(bf16[16,79,1024]{2,1,0:T(8,128)(2,1)S(1)} %get-tuple-element.218, s32[]{:T(128)S(6)} %select_n.164, f32[16,64,128]{2,1,0:T(8,128)S(1)} %get-tuple-element.207, bf16[16,1024,128]{2,1,0:T(8,128)(2,1)} %get-tuple-element.219, s32[]{:T(128)} %get-tuple-element.206, pred[]{:T(512)S(6)} %compare.18), kind=kOutput, calls=%fused_computation.2.clone.1 | convolution fusion | flops 268697600 | bytes 3408389 | tf_op jit(solution)/shard_map/while/body/eval_jaxpr/btj,js->bts/dot_general | solution.py:23
  128.5 1.7 %fusion.13 = f32[16,64,128]{2,1,0:T(8,128)S(1)} fusion(bf16[16,79,1024]{2,1,0:T(8,128)(2,1)S(1)} %get-tuple-element.218, s32[]{:T(128)S(6)} %select_n.164, f32[16,64,128]{2,1,0:T(8,128)S(1)} %get-tuple-element.207, bf16[16,1024,128]{2,1,0:T(8,128)(2,1)} %get-tuple-element.219, s32[]{:T(128)} %get-tuple-element.206, pred[]{:T(512)S(6)} %compare.18), kind=kOutput, calls=%fused_computation.2.clone.1 | convolution fusion | flops 268697600 | bytes 3408389 | tf_op jit(solution)/shard_map/while/body/eval_jaxpr/btj,js->bts/dot_general | solution.py:23
  132.1 1.7 %fusion.13 = f32[16,64,128]{2,1,0:T(8,128)S(1)} fusion(bf16[16,79,1024]{2,1,0:T(8,128)(2,1)S(1)} %get-tuple-element.218, s32[]{:T(128)S(6)} %select_n.164, f32[16,64,128]{2,1,0:T(8,128)S(1)} %get-tuple-element.207, bf16[16,1024,128]{2,1,0:T(8,128)(2,1)} %get-tuple-element.219, s32[]{:T(128)} %get-tuple-element.206, pred[]{:T(512)S(6)} %compare.18), kind=kOutput, calls=%fused_computation.2.clone.1 | convolution fusion | flops 268697600 | bytes 3408389 | tf_op jit(solution)/shard_map/while/body/eval_jaxpr/btj,js->bts/dot_general | solution.py:23
  135.8 1.7 %fusion.13 = f32[16,64,128]{2,1,0:T(8,128)S(1)} fusion(bf16[16,79,1024]{2,1,0:T(8,128)(2,1)S(1)} %get-tuple-element.218, s32[]{:T(128)S(6)} %select_n.164, f32[16,64,128]{2,1,0:T(8,128)S(1)} %get-tuple-element.207, bf16[16,1024,128]{2,1,0:T(8,128)(2,1)} %get-tuple-element.219, s32[]{:T(128)} %get-tuple-element.206, pred[]{:T(512)S(6)} %compare.18), kind=kOutput, calls=%fused_computation.2.clone.1 | convolution fusion | flops 268697600 | bytes 3408389 | tf_op jit(solution)/shard_map/while/body/eval_jaxpr/btj,js->bts/dot_general | solution.py:23
  139.4 1.7 %fusion.13 = f32[16,64,128]{2,1,0:T(8,128)S(1)} fusion(bf16[16,79,1024]{2,1,0:T(8,128)(2,1)S(1)} %get-tuple-element.218, s32[]{:T(128)S(6)} %select_n.164, f32[16,64,128]{2,1,0:T(8,128)S(1)} %get-tuple-element.207, bf16[16,1024,128]{2,1,0:T(8,128)(2,1)} %get-tuple-element.219, s32[]{:T(128)} %get-tuple-element.206, pred[]{:T(512)S(6)} %compare.18), kind=kOutput, calls=%fused_computation.2.clone.1 | convolution fusion | flops 268697600 | bytes 3408389 | tf_op jit(solution)/shard_map/while/body/eval_jaxpr/btj,js->bts/dot_general | solution.py:23
  143.1 1.7 %fusion.13 = f32[16,64,128]{2,1,0:T(8,128)S(1)} fusion(bf16[16,79,1024]{2,1,0:T(8,128)(2,1)S(1)} %get-tuple-element.218, s32[]{:T(128)S(6)} %select_n.164, f32[16,64,128]{2,1,0:T(8,128)S(1)} %get-tuple-element.207, bf16[16,1024,128]{2,1,0:T(8,128)(2,1)} %get-tuple-element.219, s32[]{:T(128)} %get-tuple-element.206, pred[]{:T(512)S(6)} %compare.18), kind=kOutput, calls=%fused_computation.2.clone.1 | convolution fusion | flops 268697600 | bytes 3408389 | tf_op jit(solution)/shard_map/while/body/eval_jaxpr/btj,js->bts/dot_general | solution.py:23
  146.8 1.7 %fusion.13 = f32[16,64,128]{2,1,0:T(8,128)S(1)} fusion(bf16[16,79,1024]{2,1,0:T(8,128)(2,1)S(1)} %get-tuple-element.218, s32[]{:T(128)S(6)} %select_n.164, f32[16,64,128]{2,1,0:T(8,128)S(1)} %get-tuple-element.207, bf16[16,1024,128]{2,1,0:T(8,128)(2,1)} %get-tuple-element.219, s32[]{:T(128)} %get-tuple-element.206, pred[]{:T(512)S(6)} %compare.18), kind=kOutput, calls=%fused_computation.2.clone.1 | convolution fusion | flops 268697600 | bytes 3408389 | tf_op jit(solution)/shard_map/while/body/eval_jaxpr/btj,js->bts/dot_general | solution.py:23
  150.4 1.7 %fusion.13 = f32[16,64,128]{2,1,0:T(8,128)S(1)} fusion(bf16[16,79,1024]{2,1,0:T(8,128)(2,1)S(1)} %get-tuple-element.218, s32[]{:T(128)S(6)} %select_n.164, f32[16,64,128]{2,1,0:T(8,128)S(1)} %get-tuple-element.207, bf16[16,1024,128]{2,1,0:T(8,128)(2,1)} %get-tuple-element.219, s32[]{:T(128)} %get-tuple-element.206, pred[]{:T(512)S(6)} %compare.18), kind=kOutput, calls=%fused_computation.2.clone.1 | convolution fusion | flops 268697600 | bytes 3408389 | tf_op jit(solution)/shard_map/while/body/eval_jaxpr/btj,js->bts/dot_general | solution.py:23
  154.1 1.7 %fusion.13 = f32[16,64,128]{2,1,0:T(8,128)S(1)} fusion(bf16[16,79,1024]{2,1,0:T(8,128)(2,1)S(1)} %get-tuple-element.218, s32[]{:T(128)S(6)} %select_n.164, f32[16,64,128]{2,1,0:T(8,128)S(1)} %get-tuple-element.207, bf16[16,1024,128]{2,1,0:T(8,128)(2,1)} %get-tuple-element.219, s32[]{:T(128)} %get-tuple-element.206, pred[]{:T(512)S(6)} %compare.18), kind=kOutput, calls=%fused_computation.2.clone.1 | convolution fusion | flops 268697600 | bytes 3408389 | tf_op jit(solution)/shard_map/while/body/eval_jaxpr/btj,js->bts/dot_general | solution.py:23
  157.7 1.7 %fusion.13 = f32[16,64,128]{2,1,0:T(8,128)S(1)} fusion(bf16[16,79,1024]{2,1,0:T(8,128)(2,1)S(1)} %get-tuple-element.218, s32[]{:T(128)S(6)} %select_n.164, f32[16,64,128]{2,1,0:T(8,128)S(1)} %get-tuple-element.207, bf16[16,1024,128]{2,1,0:T(8,128)(2,1)} %get-tuple-element.219, s32[]{:T(128)} %get-tuple-element.206, pred[]{:T(512)S(6)} %compare.18), kind=kOutput, calls=%fused_computation.2.clone.1 | convolution fusion | flops 268697600 | bytes 3408389 | tf_op jit(solution)/shard_map/while/body/eval_jaxpr/btj,js->bts/dot_general | solution.py:23
  (46 shorter events, 17.4 us)
Async XLA Ops:
  0.0 37.0 %copy-start = (bf16[16,64,128]{2,1,0:T(8,128)(2,1)S(1)}, bf16[16,64,128]{2,1,0:T(8,128)(2,1)}, u32[]{:S(2)}) copy-start(bf16[16,64,128]{2,1,0:T(8,128)(2,1)} %param.6) | copy-start | bytes 786436
  0.0 14.4 %collective-permute-start.1 = (bf16[16,64,128]{2,1,0:T(8,128)(2,1)}, bf16[16,64,128]{2,1,0:T(8,128)(2,1)S(1)}, u32[]{:S(2)}, u32[]{:S(2)}) collective-permute-start(bf16[16,64,128]{2,1,0:T(8,128)(2,1)} %param.6), channel_id=1, source_target_pairs={{0,2},{2,4},{4,6},{6,8},{8,10},{10,12},{12,14},{14,16},{16,18},{18... | collective-permute-start | bytes 786440 | tf_op jit(solution)/shard_map/ppermute | solution.py:43
  2.9 13.9 %collective-permute-start.2 = (bf16[16,64,128]{2,1,0:T(8,128)(2,1)}, bf16[16,64,128]{2,1,0:T(8,128)(2,1)S(1)}, u32[]{:S(2)}, u32[]{:S(2)}) collective-permute-start(bf16[16,64,128]{2,1,0:T(8,128)(2,1)} %param.6), channel_id=1, source_target_pairs={{0,30},{2,0},{4,2},{6,4},{8,6},{10,8},{12,10},{14,12},{16,14},{18,... | collective-permute-start | bytes 786440 | tf_op jit(solution)/shard_map/ppermute | solution.py:46
  14.4 12.7 %collective-permute-start.3 = (bf16[16,64,128]{2,1,0:T(8,128)(2,1)S(1)}, bf16[16,64,128]{2,1,0:T(8,128)(2,1)S(1)}, u32[]{:S(2)}, u32[]{:S(2)}) collective-permute-start(bf16[16,64,128]{2,1,0:T(8,128)(2,1)S(1)} %collective-permute-done.1), channel_id=1, source_target_pairs={{0,2},{2,4},{4,6},{6,8},{8,10},{10,12},{12,14},{14,16},{16,18},{18... | collective-permute-start | bytes 786440 | tf_op jit(solution)/shard_map/ppermute | solution.py:43
  16.8 12.8 %collective-permute-start.4 = (bf16[16,64,128]{2,1,0:T(8,128)(2,1)S(1)}, bf16[16,64,128]{2,1,0:T(8,128)(2,1)S(1)}, u32[]{:S(2)}, u32[]{:S(2)}) collective-permute-start(bf16[16,64,128]{2,1,0:T(8,128)(2,1)S(1)} %collective-permute-done.2), channel_id=1, source_target_pairs={{0,30},{2,0},{4,2},{6,4},{8,6},{10,8},{12,10},{14,12},{16,14},{18,... | collective-permute-start | bytes 786440 | tf_op jit(solution)/shard_map/ppermute | solution.py:46
  21.3 26.8 %collective-permute-start = (bf16[16,15,1024]{2,1,0:T(8,128)(2,1)S(1)}, bf16[16,15,1024]{2,1,0:T(8,128)(2,1)}, u32[]{:S(2)}, u32[]{:S(2)}) collective-permute-start(bf16[16,15,1024]{2,1,0:T(8,128)(2,1)S(1)} %slice.3), channel_id=1, source_target_pairs={{0,1},{2,3},{4,5},{6,7},{8,9},{10,11},{12,13},{14,15},{16,17},{18,... | collective-permute-start | bytes 1474568 | tf_op jit(solution)/shard_map/ppermute | solution.py:10
  27.1 11.9 %collective-permute-start.5 = (bf16[16,64,128]{2,1,0:T(8,128)(2,1)S(1)}, bf16[16,64,128]{2,1,0:T(8,128)(2,1)}, u32[]{:S(2)}, u32[]{:S(2)}) collective-permute-start(bf16[16,64,128]{2,1,0:T(8,128)(2,1)S(1)} %collective-permute-done.3), channel_id=1, source_target_pairs={{0,2},{2,4},{4,6},{6,8},{8,10},{10,12},{12,14},{14,16},{16,18},{18... | collective-permute-start | bytes 786440 | tf_op jit(solution)/shard_map/ppermute | solution.py:43
  29.6 18.4 %copy-start.1 = (bf16[16,64,128]{2,1,0:T(8,128)(2,1)}, bf16[16,64,128]{2,1,0:T(8,128)(2,1)S(1)}, u32[]{:S(2)}) copy-start(bf16[16,64,128]{2,1,0:T(8,128)(2,1)S(1)} %collective-permute-done.4) | copy-start | bytes 786436
  29.6 12.7 %collective-permute-start.6 = (bf16[16,64,128]{2,1,0:T(8,128)(2,1)S(1)}, bf16[16,64,128]{2,1,0:T(8,128)(2,1)}, u32[]{:S(2)}, u32[]{:S(2)}) collective-permute-start(bf16[16,64,128]{2,1,0:T(8,128)(2,1)S(1)} %collective-permute-done.4), channel_id=1, source_target_pairs={{0,30},{2,0},{4,2},{6,4},{8,6},{10,8},{12,10},{14,12},{16,14},{18,... | collective-permute-start | bytes 786440 | tf_op jit(solution)/shard_map/ppermute | solution.py:46
  39.0 12.7 %collective-permute-start.7 = (bf16[16,64,128]{2,1,0:T(8,128)(2,1)}, bf16[16,64,128]{2,1,0:T(8,128)(2,1)S(1)}, u32[]{:S(2)}, u32[]{:S(2)}) collective-permute-start(bf16[16,64,128]{2,1,0:T(8,128)(2,1)} %collective-permute-done.5), channel_id=1, source_target_pairs={{0,2},{2,4},{4,6},{6,8},{8,10},{10,12},{12,14},{14,16},{16,18},{18... | collective-permute-start | bytes 786440 | tf_op jit(solution)/shard_map/ppermute | solution.py:43
  42.3 13.3 %collective-permute-start.8 = (bf16[16,64,128]{2,1,0:T(8,128)(2,1)}, bf16[16,64,128]{2,1,0:T(8,128)(2,1)S(1)}, u32[]{:S(2)}, u32[]{:S(2)}) collective-permute-start(bf16[16,64,128]{2,1,0:T(8,128)(2,1)} %collective-permute-done.6), channel_id=1, source_target_pairs={{0,30},{2,0},{4,2},{6,4},{8,6},{10,8},{12,10},{14,12},{16,14},{18,... | collective-permute-start | bytes 786440 | tf_op jit(solution)/shard_map/ppermute | solution.py:46
  48.1 6.8 %copy-start.2 = (bf16[16,64,128]{2,1,0:T(8,128)(2,1)S(1)}, bf16[16,64,128]{2,1,0:T(8,128)(2,1)}, u32[]{:S(2)}) copy-start(bf16[16,64,128]{2,1,0:T(8,128)(2,1)} %copy-done.1) | copy-start | bytes 786436
  50.7 50.3 %copy-start.3 = (s32[16]{0:T(128)S(1)}, s32[16]{0:T(128)}, u32[]{:S(2)}) copy-start(s32[16]{0:T(128)} %param.7) | copy-start | bytes 196
  51.7 12.3 %collective-permute-start.9 = (bf16[16,64,128]{2,1,0:T(8,128)(2,1)S(1)}, bf16[16,64,128]{2,1,0:T(8,128)(2,1)S(1)}, u32[]{:S(2)}, u32[]{:S(2)}) collective-permute-start(bf16[16,64,128]{2,1,0:T(8,128)(2,1)S(1)} %collective-permute-done.7), channel_id=1, source_target_pairs={{0,2},{2,4},{4,6},{6,8},{8,10},{10,12},{12,14},{14,16},{16,18},{18... | collective-permute-start | bytes 786440 | tf_op jit(solution)/shard_map/ppermute | solution.py:43
  55.7 12.9 %collective-permute-start.10 = (bf16[16,64,128]{2,1,0:T(8,128)(2,1)S(1)}, bf16[16,64,128]{2,1,0:T(8,128)(2,1)S(1)}, u32[]{:S(2)}, u32[]{:S(2)}) collective-permute-start(bf16[16,64,128]{2,1,0:T(8,128)(2,1)S(1)} %collective-permute-done.8), channel_id=1, source_target_pairs={{0,30},{2,0},{4,2},{6,4},{8,6},{10,8},{12,10},{14,12},{16,14},{18,... | collective-permute-start | bytes 786440 | tf_op jit(solution)/shard_map/ppermute | solution.py:46
  64.1 12.6 %collective-permute-start.11 = (bf16[16,64,128]{2,1,0:T(8,128)(2,1)S(1)}, bf16[16,64,128]{2,1,0:T(8,128)(2,1)S(1)}, u32[]{:S(2)}, u32[]{:S(2)}) collective-permute-start(bf16[16,64,128]{2,1,0:T(8,128)(2,1)S(1)} %collective-permute-done.9), channel_id=1, source_target_pairs={{0,2},{2,4},{4,6},{6,8},{8,10},{10,12},{12,14},{14,16},{16,18},{18... | collective-permute-start | bytes 786440 | tf_op jit(solution)/shard_map/ppermute | solution.py:43
  68.6 12.6 %collective-permute-start.12 = (bf16[16,64,128]{2,1,0:T(8,128)(2,1)S(1)}, bf16[16,64,128]{2,1,0:T(8,128)(2,1)S(1)}, u32[]{:S(2)}, u32[]{:S(2)}) collective-permute-start(bf16[16,64,128]{2,1,0:T(8,128)(2,1)S(1)} %collective-permute-done.10), channel_id=1, source_target_pairs={{0,30},{2,0},{4,2},{6,4},{8,6},{10,8},{12,10},{14,12},{16,14},{18,... | collective-permute-start | bytes 786440 | tf_op jit(solution)/shard_map/ppermute | solution.py:46
  76.6 12.1 %collective-permute-start.13 = (bf16[16,64,128]{2,1,0:T(8,128)(2,1)S(1)}, bf16[16,64,128]{2,1,0:T(8,128)(2,1)S(1)}, u32[]{:S(2)}, u32[]{:S(2)}) collective-permute-start(bf16[16,64,128]{2,1,0:T(8,128)(2,1)S(1)} %collective-permute-done.11), channel_id=1, source_target_pairs={{0,2},{2,4},{4,6},{6,8},{8,10},{10,12},{12,14},{14,16},{16,18},{18... | collective-permute-start | bytes 786440 | tf_op jit(solution)/shard_map/ppermute | solution.py:43
  81.2 12.5 %collective-permute-start.14 = (bf16[16,64,128]{2,1,0:T(8,128)(2,1)S(1)}, bf16[16,64,128]{2,1,0:T(8,128)(2,1)S(1)}, u32[]{:S(2)}, u32[]{:S(2)}) collective-permute-start(bf16[16,64,128]{2,1,0:T(8,128)(2,1)S(1)} %collective-permute-done.12), channel_id=1, source_target_pairs={{0,30},{2,0},{4,2},{6,4},{8,6},{10,8},{12,10},{14,12},{16,14},{18,... | collective-permute-start | bytes 786440 | tf_op jit(solution)/shard_map/ppermute | solution.py:46
  88.7 11.5 %collective-permute-start.15 = (bf16[16,64,128]{2,1,0:T(8,128)(2,1)S(1)}, bf16[16,64,128]{2,1,0:T(8,128)(2,1)S(1)}, u32[]{:S(2)}, u32[]{:S(2)}) collective-permute-start(bf16[16,64,128]{2,1,0:T(8,128)(2,1)S(1)} %collective-permute-done.13), channel_id=1, source_target_pairs={{0,2},{2,4},{4,6},{6,8},{8,10},{10,12},{12,14},{14,16},{16,18},{18... | collective-permute-start | bytes 786440 | tf_op jit(solution)/shard_map/ppermute | solution.py:43
